TPU v7x, 256 devices: a whole 4x4x8 slice. The times are simulated.
256 devices in a mesh: roll: 4 (over z_lo, core), mach: 16 (over y, x), cross: 4 (over z_hi).
Axes of the slice: x: 4, y: 4, z: 8 (z_hi: 4, z_lo: 2; z = z_hi * 2 + z_lo), core: 2. Of those that a mesh axis runs over, the one named last changes fastest.
Arguments:
- density: bfloat16 [128, 4096, 2048], P('roll', 'mach', 'cross'), may hold values from 0 to 1
- roll_start: float32 [32, 128], P(None, 'roll'), may hold values from 0.05 to 1
- mach_factor: bfloat16 [32, 4096], P(None, 'mach'), may hold values from 0.0099487305 to 1
- cross_factor: bfloat16 [32, 2048], P(None, 'cross'), may hold values from 0.0099487305 to 1
Outputs:
- roll_factor: float32 [32, 128], P(None, 'roll')
- mode_two: float32 [32, 4096], P(None, ('mach', 'cross'))
All inputs are finite; a program needn't handle non-finite values.
Results may differ from a plain program's by a relative error of at most 0.0003.
Values sent between devices are 32-bit elements; how exact they have to be, the bound alone decides.
A program may use at most 64 MiB of HBM per device.

v0:
```python
import jax
import jax.numpy as jnp
from jax import lax
from jax.sharding import PartitionSpec as P


def hals_rows(roll_rows, mttkrp, gram):

    def column_step(column, rows):
        column = jnp.asarray(column).astype(jnp.int32)
        gram_row = lax.dynamic_slice_in_dim(gram, column, 1, 0)
        diag_entry = lax.dynamic_slice_in_dim(gram_row, column, 1, 1)
        current = lax.dynamic_slice_in_dim(rows, column, 1, 0)
        target = lax.dynamic_slice_in_dim(mttkrp, column, 1, 0)
        mixed = jnp.dot(gram_row, rows, precision=lax.Precision.HIGHEST)
        updated = jnp.maximum(current + (target - mixed) / diag_entry, 0.0)
        return lax.dynamic_update_slice_in_dim(rows, updated, column, 0)

    return lax.fori_loop(0, roll_rows.shape[0], column_step, roll_rows)


def local(density, roll_start, mach_factor, cross_factor):
    rolls_here, bins_here, cross_here = density.shape
    rank = cross_factor.shape[0]
    flat = density.reshape(rolls_here * bins_here, cross_here)
    partial_value = lax.dot_general(
        cross_factor, flat, (((1,), (1,)), ((), ())), preferred_element_type=jnp.float32
    )
    partial_value = partial_value.reshape(rank, rolls_here, bins_here)
    local_terms = jnp.einsum(
        "rij,rj->ri",
        partial_value,
        mach_factor.astype(jnp.float32),
        precision=lax.Precision.HIGHEST,
    )
    local_mach = jnp.dot(mach_factor, mach_factor.T, preferred_element_type=jnp.float32)
    local_cross = jnp.dot(cross_factor, cross_factor.T, preferred_element_type=jnp.float32)
    mttkrp = lax.psum(local_terms, ("mach", "cross"))
    gram_mach = lax.psum(local_mach, "mach")
    gram_cross = lax.psum(local_cross, "cross")
    gram = gram_mach * gram_cross
    roll_factor = hals_rows(roll_start, mttkrp, gram)
    term = jnp.einsum("rij,ri->rj", partial_value, roll_factor, precision=lax.Precision.HIGHEST)
    whole = lax.psum(term, ("roll", "cross"))
    span = whole.shape[1] // lax.axis_size("cross")
    total = lax.dynamic_slice_in_dim(whole, lax.axis_index("cross") * span, span, 1)
    all_rolls = rolls_here * lax.axis_size("roll")
    all_cross = cross_here * lax.axis_size("cross")
    scale = rank / (all_rolls * all_cross)
    mode_two = total * scale
    return (roll_factor, mode_two)


def solution(mesh):
    in_specs = (P("roll", "mach", "cross"), P(None, "roll"), P(None, "mach"), P(None, "cross"))
    out_specs = (P(None, "roll"), P(None, ("mach", "cross")))
    return jax.shard_map(local, mesh=mesh, in_specs=in_specs, out_specs=out_specs, check_vma=False)
```

profile of v0, /device:TPU:1, one launch (start us, length us, event | category | flops | bytes accessed | tf_op | source)
XLA Modules:
  0.0 584.9 jit_solution(14968535453906031717)
XLA Ops:
  1.4 5.9 %fusion.9 = f32[32,32,256]{2,0,1:T(8,128)S(1)} fusion(bf16[32,256,512]{2,1,0:T(8,128)(2,1)} %param.6, bf16[32,512]{1,0:T(8,128)(2,1)S(1)} %copy-done), kind=kOutput, calls=%fused_computation.12 | convolution fusion | flops 268435456 | bytes 9469952 | tf_op jit(solution)/shard_map/dot_general | solution.py:26
  7.3 1.2 fusion.7
  8.5 327.1 %psum.28 = f32[32,32]{1,0:T(8,128)S(1)} all-reduce(f32[32,32]{1,0:T(8,128)S(1)} %bitcast.34), channel_id=1, replica_groups=mesh['roll'=4,'mach'=16,'cross'=4] {'mach','cross'}, use_global_device_ids=true, to_apply=%region_2.0 | all-reduce | flops 1024 | bytes 8192 | tf_op jit(solution)/shard_map/psum | solution.py:38
  335.7 56.2 %psum.29 = f32[32,32]{1,0:T(8,128)S(1)} all-reduce(f32[32,32]{1,0:T(8,128)S(1)} %fusion.12), channel_id=1, replica_groups=mesh['roll'=4,'mach'=16,'cross'=4] {'mach'}, use_global_device_ids=true, to_apply=%region_0.0 | all-reduce | flops 1024 | bytes 8192 | tf_op jit(solution)/shard_map/psum | solution.py:39
  392.0 12.7 %psum.30 = f32[32,32]{1,0:T(8,128)S(1)} all-reduce(f32[32,32]{1,0:T(8,128)S(1)} %fusion.13), channel_id=1, replica_groups=mesh['roll'=4,'mach'=16,'cross'=4] {'cross'}, use_global_device_ids=true, to_apply=%region_1.0 | all-reduce | flops 1024 | bytes 8192 | tf_op jit(solution)/shard_map/psum | solution.py:40
  404.7 45.2 %while.16 = (s32[]{:T(128)}, f32[32,32]{1,0:T(8,128)S(1)}, f32[32,32]{1,0:T(8,128)S(1)}, f32[32,32]{1,0:T(8,128)S(1)}, s32[]{:T(128)}, /*index=5*/s32[]{:T(128)}, s32[]{:T(128)}) while((s32[]{:T(128)}, f32[32,32]{1,0:T(8,128)S(1)}, f32[32,32]{1,0:T(8,128)S(1)}, f32[32,32]{1,0:T(8,128)S(1)}, s32[]{:T(128)}, /*index=5*/s32[]{:T(128)}, ...), condition=%wide.region_4.0_spmd, body=%wide.region_3.0_spmd.sunk | while | flops 12419 | bytes 19449 | solution.py:19
  405.3 0.8 fusion.26
  406.7 0.8 fusion.26
  408.1 0.8 fusion.26
  409.6 0.8 fusion.26
  411.0 0.8 fusion.26
  412.4 0.8 fusion.26
  413.8 0.8 fusion.26
  415.2 0.8 fusion.26
  416.6 0.8 fusion.26
  418.0 0.8 fusion.26
  419.4 0.8 fusion.26
  420.8 0.8 fusion.26
  422.3 0.8 fusion.26
  423.7 0.8 fusion.26
  425.1 0.8 fusion.26
  426.5 0.8 fusion.26
  429.3 0.8 fusion.26
  430.7 0.8 fusion.26
  432.1 0.8 fusion.26
  433.6 0.8 fusion.26
  435.0 0.8 fusion.26
  436.4 0.8 fusion.26
  437.8 0.8 fusion.26
  439.2 0.8 fusion.26
  449.9 1.3 fusion.5
  451.2 133.1 %psum.31 = f32[32,256]{1,0:T(8,128)S(1)} all-reduce(f32[32,256]{1,0:T(8,128)S(1)} %bitcast.33), channel_id=1, replica_groups=mesh['roll'=4,'mach'=16,'cross'=4] {'roll','cross'}, use_global_device_ids=true, to_apply=%region_5.0 | all-reduce | flops 8192 | bytes 65536 | tf_op jit(solution)/shard_map/psum | solution.py:44
  (85 shorter events, 27.6 us)
Async XLA Ops:
  0.6 0.8 copy-start
  0.6 404.1 %copy-start.2 = (f32[32,32]{1,0:T(8,128)S(1)}, f32[32,32]{1,0:T(8,128)}, u32[]{:S(2)}) copy-start(f32[32,32]{1,0:T(8,128)} %param.7) | copy-start | bytes 12292
  0.7 6.6 %copy-start.3 = (bf16[32,256]{1,0:T(8,128)(2,1)S(1)}, bf16[32,256]{1,0:T(8,128)(2,1)}, u32[]{:S(2)}) copy-start(bf16[32,256]{1,0:T(8,128)(2,1)} %param.8) | copy-start | bytes 49156
  449.9 135.0 %copy-start.1 = (f32[32,32]{1,0:T(8,128)}, f32[32,32]{1,0:T(8,128)S(1)}, u32[]{:S(2)}) copy-start(f32[32,32]{1,0:T(8,128)S(1)} %get-tuple-element.124) | copy-start | bytes 12292
where the time goes:
time: 585 us
  blocking collectives  529 us (90%)
  matrix products  33.6 us (6%)
  local copies, waits for them, and re-layouts  20.4 us (3%)
    psum x1, blocking collectives, local(): mttkrp = lax.psum(local_terms, ('mach', 'cross'))  327 us
    psum x1, blocking collectives, local(): whole = lax.psum(term, ('roll', 'cross'))  133 us
    psum x1, blocking collectives, local(): gram_mach = lax.psum(local_mach, 'mach')  56.2 us
    dot_general x32, matrix products, column_step(): mixed = jnp.dot(gram_row, rows, precision=lax.Precision.HIGHEST)  25 us
    dynamic_slice x32, local copies, waits for them, and re-layouts, column_step(): diag_entry = lax.dynamic_slice_in_dim(gram_row, column, 1, 1)  18.8 us
    psum x1, blocking collectives, local(): gram_cross = lax.psum(local_cross, 'cross')  12.7 us

commit v1 on v0

--- a/solution.py
+++ b/solution.py
@@ -2,6 +2,19 @@
 import jax.numpy as jnp
 from jax import lax
 from jax.sharding import PartitionSpec as P
+from jax.lax import axis_size, ppermute
+
+
+def _begin_pipes(message, lane_axis):
+    wide_n = axis_size(lane_axis)
+    row_out = message
+    for jj in [at for at in (1, 2, 4, 8, 16) if at < wide_n]:
+        crops = []
+        for hop_no in [*range(wide_n)]:
+            crops.append((hop_no, hop_no ^ jj))
+        v_next = ppermute(row_out, lane_axis, crops)
+        row_out = row_out + v_next
+    return row_out
 
 
 def hals_rows(roll_rows, mttkrp, gram):
@@ -36,7 +49,7 @@
     local_mach = jnp.dot(mach_factor, mach_factor.T, preferred_element_type=jnp.float32)
     local_cross = jnp.dot(cross_factor, cross_factor.T, preferred_element_type=jnp.float32)
     mttkrp = lax.psum(local_terms, ("mach", "cross"))
-    gram_mach = lax.psum(local_mach, "mach")
+    gram_mach = _begin_pipes(local_mach, "mach")
     gram_cross = lax.psum(local_cross, "cross")
     gram = gram_mach * gram_cross
     roll_factor = hals_rows(roll_start, mttkrp, gram)

time: 585 us -> 521 us (0.89)
  blocking collectives: 529 us -> 454 us
  starting transfers between devices: 0 us -> 8.58 us
    psum x1 -> x0, blocking collectives: 56.2 us -> none  [local(): gram_mach = lax.psum(local_mach, 'mach')]
    psum x1, blocking collectives: 133 us -> 119 us  [local(): whole = lax.psum(term, ('roll', 'cross'))]
    psum x1, blocking collectives: 327 us -> 317 us  [local(): mttkrp = lax.psum(local_terms, ('mach', 'cross'))]
    ppermute x0 -> x4, starting transfers between devices: none -> 8.58 us  [_begin_pipes(): v_next = ppermute(row_out, lane_axis, crops)]
  transfers between devices with their start and end apart: 0 -> 4, of which waited for: 0 -> 1; matrix products, arithmetic and copies ran while one was open for 0% -> 1% of each run, Pallas kernels for 0% -> 0%
where the time goes in v1:
time: 521 us
  blocking collectives  454 us (87%)
  matrix products  34.4 us (7%)
  local copies, waits for them, and re-layouts  19.7 us (4%)
  starting transfers between devices  8.58 us (2%)
    psum x1, blocking collectives, local(): mttkrp = lax.psum(local_terms, ('mach', 'cross'))  317 us
    psum x1, blocking collectives, local(): whole = lax.psum(term, ('roll', 'cross'))  119 us
    dot_general x32, matrix products, column_step(): mixed = jnp.dot(gram_row, rows, precision=lax.Precision.HIGHEST)  25 us
    dynamic_slice x32, local copies, waits for them, and re-layouts, column_step(): diag_entry = lax.dynamic_slice_in_dim(gram_row, column, 1, 1)  18.8 us
    psum x1, blocking collectives, local(): gram_cross = lax.psum(local_cross, 'cross')  18.5 us
  transfers between devices with their start and end apart: 4, of which 1 were waited for; matrix products, arithmetic and copies ran while one was open for 1% of the time, Pallas kernels for 0%

profile of v1, /device:TPU:1, one launch (start us, length us, event | category | flops | bytes accessed | tf_op | source)
XLA Modules:
  0.0 520.6 jit_solution(14580374367611063691)
XLA Ops:
  0.7 0.9 fusion.12
  1.6 2.0 collective-permute-start
  3.6 5.9 %fusion.9 = f32[32,32,256]{2,0,1:T(8,128)S(1)} fusion(bf16[32,256,512]{2,1,0:T(8,128)(2,1)} %param.6, bf16[32,512]{1,0:T(8,128)(2,1)S(1)} %copy-done), kind=kOutput, calls=%fused_computation.12 | convolution fusion | flops 268435456 | bytes 9469952 | tf_op jit(solution)/shard_map/dot_general | solution.py:39
  9.6 1.2 fusion.7
  10.8 2.5 collective-permute-start.1
  13.4 1.5 collective-permute-done.1
  14.9 1.3 collective-permute-start.2
  16.2 18.5 %psum.22 = f32[32,32]{1,0:T(8,128)S(1)} all-reduce(f32[32,32]{1,0:T(8,128)S(1)} %fusion.13), channel_id=1, replica_groups=mesh['roll'=4,'mach'=16,'cross'=4] {'cross'}, use_global_device_ids=true, to_apply=%region_0.0 | all-reduce | flops 1024 | bytes 8192 | tf_op jit(solution)/shard_map/psum | solution.py:53
  34.7 2.7 collective-permute-start.3
  37.4 316.6 %psum.21 = f32[32,32]{1,0:T(8,128)S(1)} all-reduce(f32[32,32]{1,0:T(8,128)S(1)} %bitcast.34), channel_id=1, replica_groups=mesh['roll'=4,'mach'=16,'cross'=4] {'mach','cross'}, use_global_device_ids=true, to_apply=%region_1.0 | all-reduce | flops 1024 | bytes 8192 | tf_op jit(solution)/shard_map/psum | solution.py:51
  354.0 45.2 %while.16 = (s32[]{:T(128)}, f32[32,32]{1,0:T(8,128)S(1)}, f32[32,32]{1,0:T(8,128)S(1)}, f32[32,32]{1,0:T(8,128)S(1)}, s32[]{:T(128)}, /*index=5*/s32[]{:T(128)}, s32[]{:T(128)}) while((s32[]{:T(128)}, f32[32,32]{1,0:T(8,128)S(1)}, f32[32,32]{1,0:T(8,128)S(1)}, f32[32,32]{1,0:T(8,128)S(1)}, s32[]{:T(128)}, /*index=5*/s32[]{:T(128)}, ...), condition=%wide.region_3.0_spmd, body=%wide.region_2.0_spmd.sunk | while | flops 12419 | bytes 19949 | solution.py:32
  354.6 0.8 fusion.26
  356.0 0.8 fusion.26
  357.5 0.8 fusion.26
  358.9 0.8 fusion.26
  360.3 0.8 fusion.26
  361.7 0.8 fusion.26
  363.1 0.8 fusion.26
  364.5 0.8 fusion.26
  365.9 0.8 fusion.26
  367.3 0.8 fusion.26
  368.7 0.8 fusion.26
  371.6 0.8 fusion.26
  373.0 0.8 fusion.26
  374.4 0.8 fusion.26
  375.8 0.8 fusion.26
  377.2 0.8 fusion.26
  378.6 0.8 fusion.26
  380.0 0.8 fusion.26
  381.4 0.8 fusion.26
  399.2 1.3 fusion.5
  400.5 119.4 %psum.23 = f32[32,256]{1,0:T(8,128)S(1)} all-reduce(f32[32,256]{1,0:T(8,128)S(1)} %bitcast.33), channel_id=1, replica_groups=mesh['roll'=4,'mach'=16,'cross'=4] {'roll','cross'}, use_global_device_ids=true, to_apply=%region_4.0 | all-reduce | flops 8192 | bytes 65536 | tf_op jit(solution)/shard_map/psum | solution.py:57
  (95 shorter events, 30.7 us)
Async XLA Ops:
  0.6 3.0 copy-start
  0.6 8.9 %copy-start.3 = (bf16[32,256]{1,0:T(8,128)(2,1)S(1)}, bf16[32,256]{1,0:T(8,128)(2,1)}, u32[]{:S(2)}) copy-start(bf16[32,256]{1,0:T(8,128)(2,1)} %param.8) | copy-start | bytes 49156
  0.7 353.4 %copy-start.2 = (f32[32,32]{1,0:T(8,128)S(1)}, f32[32,32]{1,0:T(8,128)}, u32[]{:S(2)}) copy-start(f32[32,32]{1,0:T(8,128)} %param.7) | copy-start | bytes 12292
  1.6 9.2 %collective-permute-start = (f32[32,32]{1,0:T(8,128)S(1)}, f32[32,32]{1,0:T(8,128)S(1)}, u32[]{:S(2)}, u32[]{:S(2)}) collective-permute-start(f32[32,32]{1,0:T(8,128)S(1)} %fusion.12), channel_id=1, source_target_pairs={{0,4},{4,0},{8,12},{12,8},{16,20},{20,16},{24,28},{28,24},{32,36},... | collective-permute-start | bytes 12296 | tf_op jit(solution)/shard_map/ppermute | solution.py:15
  10.8 4.2 collective-permute-start.1
  14.9 19.8 %collective-permute-start.2 = (f32[32,32]{1,0:T(8,128)S(1)}, f32[32,32]{1,0:T(8,128)S(1)}, u32[]{:S(2)}, u32[]{:S(2)}) collective-permute-start(f32[32,32]{1,0:T(8,128)S(1)} %add.79), channel_id=1, source_target_pairs={{0,16},{4,20},{8,24},{12,28},{16,0},{20,4},{24,8},{28,12},{32,48},... | collective-permute-start | bytes 12296 | tf_op jit(solution)/shard_map/ppermute | solution.py:15
  34.7 319.3 %collective-permute-start.3 = (f32[32,32]{1,0:T(8,128)S(1)}, f32[32,32]{1,0:T(8,128)S(1)}, u32[]{:S(2)}, u32[]{:S(2)}) collective-permute-start(f32[32,32]{1,0:T(8,128)S(1)} %add.80), channel_id=1, source_target_pairs={{0,32},{4,36},{8,40},{12,44},{16,48},{20,52},{24,56},{28,60},{32,0... | collective-permute-start | bytes 12296 | tf_op jit(solution)/shard_map/ppermute | solution.py:15
  399.2 121.4 %copy-start.1 = (f32[32,32]{1,0:T(8,128)}, f32[32,32]{1,0:T(8,128)S(1)}, u32[]{:S(2)}) copy-start(f32[32,32]{1,0:T(8,128)S(1)} %get-tuple-element.124) | copy-start | bytes 12292
